TPU v7x, 32 devices: a whole 2x2x4 slice. The times are simulated.
32 devices in a mesh: facet: 8 (over y, x, core), sub: 4 (over z).
Axes of the slice: x: 2, y: 2, z: 4, core: 2. Of those that a mesh axis runs over, the one named last changes fastest.
Arguments:
- facet_spec: bfloat16 [8, 2, 704, 448], P('facet'), may hold values from -3 to 3
- worker_of_subgrid: int32 [32], replicated, may hold values from 0 to 31, each once
- vis_count: int32 [32], P(('facet', 'sub')), may hold values from 512 to 8192, as said below
- bin_offsets: int32 [32, 2, 8192], P(('facet', 'sub')), may hold values from 0 to 248
- bin_fractions: float32 [32, 2, 8192], P(('facet', 'sub')), may hold values from 0 to 1
- observed: float32 [32, 2, 8192], P(('facet', 'sub')), may hold values from -6 to 6
Outputs:
- residual_vis: float32 [32, 2, 8192], P(('facet', 'sub'))
- facet_update: float32 [8, 2, 704, 448], P('facet', None, 'sub')
Inputs may be any that keep to these rules, and one draw needn't show every extreme that they name: `worker_of_subgrid`: a permutation of the subgrids. `vis_count`: some device row has all 8192 slots live in every draw.
All inputs are finite; a program needn't handle non-finite values.
Results may differ from a plain program's by a relative error of at most 0.014.
Values may be sent and summed in bfloat16 or wider, within the bound.
A program may use at most 128 MiB of HBM per device.

v0:
```python
import math

import jax
import jax.numpy as jnp
from jax import lax
from jax.sharding import PartitionSpec as P

SUB = 256
MC = 256
STEP = 64
KS = 8
VB = 512


TWO_PI = 2.0 * math.pi


def phase_table(offset, facets, swapped, conj_sign):
    sub_index = jnp.arange(SUB, dtype=jnp.int32) - SUB // 2
    win_index = jnp.arange(MC, dtype=jnp.int32) - MC // 2
    if swapped:
        sub_part = sub_index[None, :]
        win_part = win_index[:, None]
    else:
        sub_part = sub_index[:, None]
        win_part = win_index[None, :]
    modulus = SUB * facets
    residue = jnp.mod(sub_part * win_part * facets + sub_part * offset, modulus)
    angles = residue.astype(jnp.float32) * (TWO_PI / modulus)
    factor = MC ** (-0.5)
    return jnp.stack([jnp.cos(angles) * factor, conj_sign * jnp.sin(angles) * factor]).astype(
        jnp.bfloat16
    )


def pair_dot(first_pair, second_pair):
    real_real = jnp.dot(first_pair[0], second_pair[0], preferred_element_type=jnp.float32)
    imag_imag = jnp.dot(first_pair[1], second_pair[1], preferred_element_type=jnp.float32)
    real_imag = jnp.dot(first_pair[0], second_pair[1], preferred_element_type=jnp.float32)
    imag_real = jnp.dot(first_pair[1], second_pair[0], preferred_element_type=jnp.float32)
    return jnp.stack([real_real - imag_imag, real_imag + imag_real])


def kernel_rows(offsets, fractions):
    cells = jnp.arange(SUB, dtype=jnp.int32)[None, :] - offsets[:, None]
    distance = cells.astype(jnp.float32) - fractions[:, None] - (0.5 * KS - 1.0)
    inside = (cells >= 0) & (cells < KS)
    weights = jnp.where(inside, 0.5 * jnp.exp(-jnp.square(distance * (9.0 / KS))), 0.0)
    return weights.astype(jnp.bfloat16)


def subgrid_holder(worker):
    total_rows = worker.shape[0]
    slot_ids = jnp.arange(total_rows, dtype=jnp.int32)
    matches = (worker[None, :] == slot_ids[:, None]).astype(jnp.int32)
    return jnp.sum(matches * slot_ids[None, :], axis=1)


def corner_of(subgrid, pos_v):
    top_row = subgrid // pos_v * STEP
    left_col = subgrid % pos_v * STEP
    return (top_row, left_col)


def window_of(spectrum, subgrid, pos_v):
    top_row, left_col = corner_of(subgrid, pos_v)
    return lax.dynamic_slice(spectrum, (jnp.int32(0), top_row, left_col), (2, MC, MC))


def add_window(plane, window, subgrid, pos_v):
    top_row, left_col = corner_of(subgrid, pos_v)
    anchor = jnp.int32(0)
    current = lax.dynamic_slice(plane, (anchor, top_row, left_col), (2, MC, MC))
    return lax.dynamic_update_slice(
        plane, current + window.astype(jnp.float32), (anchor, top_row, left_col)
    )


def grid_from(incoming, facets):

    def add_facet(running, member):
        contribution, facet_id = member
        left_table = phase_table(facet_id, facets, False, 1.0)
        right_table = phase_table(jnp.mod(5 * facet_id + 3, facets), facets, True, 1.0)
        partial_value = pair_dot(left_table, contribution).astype(jnp.bfloat16)
        return (running + pair_dot(partial_value, right_table), None)

    starting = jnp.zeros((2, SUB, SUB), jnp.float32)
    running, _ = lax.scan(add_facet, starting, (incoming, jnp.arange(facets, dtype=jnp.int32)))
    return running


def adjoint_window(resid_grid, facet_id, facets):
    left_table = phase_table(facet_id, facets, True, -1.0)
    right_table = phase_table(jnp.mod(5 * facet_id + 3, facets), facets, False, -1.0)
    partial_value = pair_dot(left_table, resid_grid).astype(jnp.bfloat16)
    return pair_dot(partial_value, right_table).astype(jnp.bfloat16)


def degrid_rows(grid_cat, offsets, fractions, observed_rows, live_count):
    slot_total = offsets.shape[1]
    blocks = (live_count + VB - 1) // VB

    def block_step(block_id, carried):
        residual, gridded = carried
        first_slot = (block_id * VB).astype(jnp.int32)
        block_offsets = lax.dynamic_slice_in_dim(offsets, first_slot, VB, 1)
        block_fractions = lax.dynamic_slice_in_dim(fractions, first_slot, VB, 1)
        block_observed = lax.dynamic_slice_in_dim(observed_rows, first_slot, VB, 1)
        u_weights = kernel_rows(block_offsets[0], block_fractions[0])
        v_weights = kernel_rows(block_offsets[1], block_fractions[1])
        product = jnp.dot(u_weights, grid_cat, preferred_element_type=jnp.float32)
        v_float = v_weights.astype(jnp.float32)
        model_real = jnp.sum(product[:, :SUB] * v_float, axis=1)
        model_imag = jnp.sum(product[:, SUB:] * v_float, axis=1)
        live_mask = first_slot + jnp.arange(VB, dtype=jnp.int32) < live_count
        real_part = jnp.where(live_mask, block_observed[0] - model_real, 0.0)
        imag_part = jnp.where(live_mask, block_observed[1] - model_imag, 0.0)
        residual = lax.dynamic_update_slice_in_dim(
            residual, jnp.stack([real_part, imag_part]), first_slot, 1
        )
        weighted = jnp.concatenate(
            [real_part[:, None] * v_float, imag_part[:, None] * v_float], axis=1
        ).astype(jnp.bfloat16)
        gridded = gridded + lax.dot_general(
            u_weights, weighted, (((0,), (0,)), ((), ())), preferred_element_type=jnp.float32
        )
        return (residual, gridded)

    starting = (jnp.zeros((2, slot_total), jnp.float32), jnp.zeros((SUB, 2 * SUB), jnp.float32))
    return lax.fori_loop(0, blocks, block_step, starting)


def on_device(facet_spec, worker_of_subgrid, vis_count, bin_offsets, bin_fractions, observed):
    sub_rank = lax.axis_index("sub")
    pos_u = lax.axis_size("facet")
    pos_v = lax.axis_size("sub")
    holder = subgrid_holder(worker_of_subgrid)
    targets = holder[jnp.arange(pos_u, dtype=jnp.int32) * pos_v + sub_rank]
    own_facet = facet_spec[0]

    def own_window(subgrid):
        return window_of(own_facet, subgrid, pos_v)

    outgoing = jax.vmap(own_window)(targets)
    incoming = lax.all_to_all(outgoing, "facet", split_axis=0, concat_axis=0, tiled=True)
    grid_sum = grid_from(incoming, pos_u)
    grid_half = grid_sum.astype(jnp.bfloat16)
    grid_cat = jnp.concatenate([grid_half[0], grid_half[1]], axis=1)
    residual, gridded = degrid_rows(
        grid_cat, bin_offsets[0], bin_fractions[0], observed[0], vis_count[0]
    )
    residual = residual[None]
    resid_grid = jnp.stack([gridded[:, :SUB], gridded[:, SUB:]]).astype(jnp.bfloat16)

    def one_window(facet_id):
        return adjoint_window(resid_grid, facet_id, pos_u)

    windows = lax.map(one_window, jnp.arange(pos_u, dtype=jnp.int32))
    returned = lax.all_to_all(windows, "facet", split_axis=0, concat_axis=0, tiled=True)
    plane_rows = facet_spec.shape[2]
    plane_cols = facet_spec.shape[3]
    plane = jnp.zeros((2, plane_rows, plane_cols), jnp.float32)

    def place_one(source, state):
        return add_window(state, returned[source], targets[source], pos_v)

    plane = lax.fori_loop(0, pos_u, place_one, plane)
    update = lax.psum_scatter(plane, "sub", scatter_dimension=1, tiled=True)
    return (residual, update[None])


def solution(mesh):
    placed = (
        P("facet", None, None, None),
        P(),
        P(("facet", "sub")),
        P(("facet", "sub"), None, None),
        P(("facet", "sub"), None, None),
        P(("facet", "sub"), None, None),
    )
    return jax.shard_map(
        on_device,
        mesh=mesh,
        in_specs=placed,
        out_specs=(P(("facet", "sub"), None, None), P("facet", None, "sub", None)),
        check_vma=False,
    )
```

profile of v0, /device:TPU:8, one launch (start us, length us, event | category | flops | bytes accessed | tf_op | source)
XLA Modules:
  0.0 539.8 jit_solution(3547265467139942495)
XLA Ops:
  11.8 22.1 %while.61 = (s32[]{:T(128)}, bf16[2,704,448]{2,1,0:T(8,128)(2,1)S(1)}, s32[8,3]{0,1:T(4,128)S(1)}, bf16[8,2,256,256]{3,2,1,0:T(8,128)(2,1)}, s32[]{:T(128)}) while((s32[]{:T(128)}, bf16[2,704,448]{2,1,0:T(8,128)(2,1)S(1)}, s32[8,3]{0,1:T(4,128)S(1)}, bf16[8,2,256,256]{3,2,1,0:T(8,128)(2,1)}, s32[]{:T(128)}) %tuple.177), condition=%wide.while_cond, body=%wide.while_body.sunk | while | flops 2 | bytes 525429 | solution.py:67
  18.0 2.1 bitcast_dynamic-update-slice_fusion.2
  20.8 2.2 bitcast_dynamic-update-slice_fusion.2
  23.5 2.2 bitcast_dynamic-update-slice_fusion.2
  26.3 2.1 bitcast_dynamic-update-slice_fusion.2
  29.1 2.1 bitcast_dynamic-update-slice_fusion.2
  31.8 2.2 bitcast_dynamic-update-slice_fusion.2
  34.0 3.7 all-to-all-start
  38.4 25.9 %all-to-all-done = bf16[8,2,256,256]{3,2,1,0:T(8,128)(2,1)S(1)} async-done(((bf16[8,2,256,256]{3,2,1,0:T(8,128)(2,1)}), bf16[8,2,256,256]{3,2,1,0:T(8,128)(2,1)S(1)}, u32[]{:S(2)}, u32[]{:S(2)}) %all-to-all-start) | async-done | bytes 2097184 | tf_op jit(solution)/shard_map/all_to_all | solution.py:146
  64.3 92.4 %while.62 = (s32[]{:T(128)}, f32[2,256,256]{2,1,0:T(8,128)S(1)}, s32[8]{0:T(128)S(1)}, bf16[8,2,256,256]{3,2,1,0:T(8,128)(2,1)S(1)}, s32[]{:T(128)}, /*index=5*/...) while((s32[]{:T(128)}, f32[2,256,256]{2,1,0:T(8,128)S(1)}, ...), condition=%wide.region_2.3_spmd.clone, body=%wide.region_1.2_spmd.clone.sunk | while | flops 278660096 | bytes 5528892 | solution.py:89
  156.9 86.6 %while.58 = (s32[]{:T(128)}, f32[2,8192]{1,0:T(2,128)S(1)}, f32[256,512]{1,0:T(8,128)S(1)}, s32[]{:T(128)}, s32[]{:T(128)}, /*index=5*/f32[2,8192]{1,0:T(2,128)}...) while((s32[]{:T(128)}, f32[2,8192]{1,0:T(2,128)S(1)}, ...), condition=%wide.region_6.7_spmd, body=%wide.region_3.6_spmd.sunk | while | flops 277747712 | bytes 4534507 | solution.py:131
  245.2 98.2 %while.59 = (s32[]{:T(128)}, bf16[8,2,256,256]{3,2,1,0:T(8,128)(2,1)}, s32[8]{0:T(128)S(1)}, bf16[2,256,256]{2,1,0:T(8,128)(2,1)S(1)}, s32[]{:T(128)}, /*index=5...) while((s32[]{:T(128)}, bf16[8,2,256,256]{3,2,1,0:T(8,128)(2,1)}, s32[8]{0:T(128)S(1)}, ...), condition=%wide.region_8.9_spmd, body=%wide.region_7.8_spmd.sunk | while | flops 278922240 | bytes 4218122 | solution.py:159
  343.4 4.4 all-to-all-start.1
  347.8 26.6 %all-to-all-done.1 = bf16[8,2,256,256]{3,2,1,0:T(8,128)(2,1)} async-done(((bf16[8,2,256,256]{3,2,1,0:T(8,128)(2,1)}), bf16[8,2,256,256]{3,2,1,0:T(8,128)(2,1)}, u32[]{:S(2)}, u32[]{:S(2)}) %all-to-all-start.1) | async-done | bytes 2097184 | tf_op jit(solution)/shard_map/all_to_all | solution.py:160
  374.8 103.6 %while.60 = (s32[]{:T(128)}, f32[2,704,448]{2,1,0:T(8,128)S(1)}, s32[8]{0:T(128)S(1)}, bf16[8,2,256,256]{3,2,1,0:T(8,128)(2,1)}, s32[]{:T(128)}, /*index=5*/s32[...) while((s32[]{:T(128)}, f32[2,704,448]{2,1,0:T(8,128)S(1)}, ...), condition=%wide.region_10.11_spmd, body=%wide.region_9.10_spmd.sunk | while | flops 262173 | bytes 2359736 | solution.py:168
  379.0 9.1 %dynamic_update_slice.32 = f32[2,704,448]{2,1,0:T(8,128)S(1)} dynamic-update-slice(f32[2,704,448]{2,1,0:T(8,128)S(1)} %get-tuple-element.851, f32[2,256,256]{2,1,0:T(8,128)S(1)} %convert_add_fusion.2, s32[]{:T(128)} %constant.406.clone.1..sunk.2, s32[]{:T(128)S(6)} %select_n.453, s32[]{:T(128)S(6)} %select_n.455) | dynamic-update-slice | bytes 1048580 | tf_op jit(solution)/shard_map/while/body/eval_jaxpr/dynamic_update_slice | solution.py:74
  392.4 7.8 %dynamic_update_slice.32 = f32[2,704,448]{2,1,0:T(8,128)S(1)} dynamic-update-slice(f32[2,704,448]{2,1,0:T(8,128)S(1)} %get-tuple-element.851, f32[2,256,256]{2,1,0:T(8,128)S(1)} %convert_add_fusion.2, s32[]{:T(128)} %constant.406.clone.1..sunk.2, s32[]{:T(128)S(6)} %select_n.453, s32[]{:T(128)S(6)} %select_n.455) | dynamic-update-slice | bytes 1048580 | tf_op jit(solution)/shard_map/while/body/eval_jaxpr/dynamic_update_slice | solution.py:74
  404.5 7.2 %dynamic_update_slice.32 = f32[2,704,448]{2,1,0:T(8,128)S(1)} dynamic-update-slice(f32[2,704,448]{2,1,0:T(8,128)S(1)} %get-tuple-element.851, f32[2,256,256]{2,1,0:T(8,128)S(1)} %convert_add_fusion.2, s32[]{:T(128)} %constant.406.clone.1..sunk.2, s32[]{:T(128)S(6)} %select_n.453, s32[]{:T(128)S(6)} %select_n.455) | dynamic-update-slice | bytes 1048580 | tf_op jit(solution)/shard_map/while/body/eval_jaxpr/dynamic_update_slice | solution.py:74
  416.0 10.8 %dynamic_update_slice.32 = f32[2,704,448]{2,1,0:T(8,128)S(1)} dynamic-update-slice(f32[2,704,448]{2,1,0:T(8,128)S(1)} %get-tuple-element.851, f32[2,256,256]{2,1,0:T(8,128)S(1)} %convert_add_fusion.2, s32[]{:T(128)} %constant.406.clone.1..sunk.2, s32[]{:T(128)S(6)} %select_n.453, s32[]{:T(128)S(6)} %select_n.455) | dynamic-update-slice | bytes 1048580 | tf_op jit(solution)/shard_map/while/body/eval_jaxpr/dynamic_update_slice | solution.py:74
  431.0 9.5 %dynamic_update_slice.32 = f32[2,704,448]{2,1,0:T(8,128)S(1)} dynamic-update-slice(f32[2,704,448]{2,1,0:T(8,128)S(1)} %get-tuple-element.851, f32[2,256,256]{2,1,0:T(8,128)S(1)} %convert_add_fusion.2, s32[]{:T(128)} %constant.406.clone.1..sunk.2, s32[]{:T(128)S(6)} %select_n.453, s32[]{:T(128)S(6)} %select_n.455) | dynamic-update-slice | bytes 1048580 | tf_op jit(solution)/shard_map/while/body/eval_jaxpr/dynamic_update_slice | solution.py:74
  444.8 9.1 %dynamic_update_slice.32 = f32[2,704,448]{2,1,0:T(8,128)S(1)} dynamic-update-slice(f32[2,704,448]{2,1,0:T(8,128)S(1)} %get-tuple-element.851, f32[2,256,256]{2,1,0:T(8,128)S(1)} %convert_add_fusion.2, s32[]{:T(128)} %constant.406.clone.1..sunk.2, s32[]{:T(128)S(6)} %select_n.453, s32[]{:T(128)S(6)} %select_n.455) | dynamic-update-slice | bytes 1048580 | tf_op jit(solution)/shard_map/while/body/eval_jaxpr/dynamic_update_slice | solution.py:74
  458.2 9.5 %dynamic_update_slice.32 = f32[2,704,448]{2,1,0:T(8,128)S(1)} dynamic-update-slice(f32[2,704,448]{2,1,0:T(8,128)S(1)} %get-tuple-element.851, f32[2,256,256]{2,1,0:T(8,128)S(1)} %convert_add_fusion.2, s32[]{:T(128)} %constant.406.clone.1..sunk.2, s32[]{:T(128)S(6)} %select_n.453, s32[]{:T(128)S(6)} %select_n.455) | dynamic-update-slice | bytes 1048580 | tf_op jit(solution)/shard_map/while/body/eval_jaxpr/dynamic_update_slice | solution.py:74
  471.9 6.5 %dynamic_update_slice.32 = f32[2,704,448]{2,1,0:T(8,128)S(1)} dynamic-update-slice(f32[2,704,448]{2,1,0:T(8,128)S(1)} %get-tuple-element.851, f32[2,256,256]{2,1,0:T(8,128)S(1)} %convert_add_fusion.2, s32[]{:T(128)} %constant.406.clone.1..sunk.2, s32[]{:T(128)S(6)} %select_n.453, s32[]{:T(128)S(6)} %select_n.455) | dynamic-update-slice | bytes 1048580 | tf_op jit(solution)/shard_map/while/body/eval_jaxpr/dynamic_update_slice | solution.py:74
  480.0 53.0 %reduce-scatter.2.cloned.1.call-done = f32[2,176,448]{2,1,0:T(8,128)} async-done(((f32[2,704,448]{2,1,0:T(8,128)}), f32[2,176,448]{2,1,0:T(8,128)}) %reduce-scatter.2.cloned.1.call-update) | async-done | bytes 630800 | tf_op jit(solution)/shard_map/reduce_scatter | solution.py:169
  (398 shorter events, 297.2 us)
Async XLA Ops:
  34.0 30.3 %all-to-all-start = ((bf16[8,2,256,256]{3,2,1,0:T(8,128)(2,1)}), bf16[8,2,256,256]{3,2,1,0:T(8,128)(2,1)S(1)}, u32[]{:S(2)}, u32[]{:S(2)}) async-start(bf16[8,2,256,256]{3,2,1,0:T(8,128)(2,1)} %get-tuple-element.427), calls=%async_computation | async-start | bytes 4194304 | tf_op jit(solution)/shard_map/all_to_all | solution.py:146
  243.5 1.7 copy-start.1
  343.4 31.0 %all-to-all-start.1 = ((bf16[8,2,256,256]{3,2,1,0:T(8,128)(2,1)}), bf16[8,2,256,256]{3,2,1,0:T(8,128)(2,1)}, u32[]{:S(2)}, u32[]{:S(2)}) async-start(bf16[8,2,256,256]{3,2,1,0:T(8,128)(2,1)} %get-tuple-element.418), calls=%async_computation.1 | async-start | bytes 4194304 | tf_op jit(solution)/shard_map/all_to_all | solution.py:160
  347.8 185.2 %reduce-scatter.2.cloned.1.call-start = ((), (), s32[]{:S(2)}) async-start(), calls=%async_computation.3 | async-start | bytes 3604480 | tf_op jit(solution)/shard_map/reduce_scatter | solution.py:169
  478.4 1.6 copy-start
Sparse Core Ops, SparseCore 0:
  480.1 52.8 reduce-scatter.1
where the time goes:
time: 546 us; the launch traced here: 540 us
  matrix products  168 us (31%)
  local copies, waits for them, and re-layouts  140 us (26%)
  waiting for transfers between devices  105 us (19%)
  other arithmetic  71.4 us (13%)
  loops' own time  31.8 us (6%)
  between operations  14.9 us (3%)
  starting transfers between devices  8.11 us (1%)
    dynamic_update_slice x8, local copies, waits for them, and re-layouts, add_window(): lax.dynamic_update_slice(plane, current + window.astype(jnp.float32), (an...  69.5 us
    reduce_scatter x1, waiting for transfers between devices, on_device(): update = lax.psum_scatter(plane, 'sub', scatter_dimension=1, tiled=True)  53 us
    dot_general x32, matrix products, pair_dot(): jnp.dot(first_pair[1], second_pair[1], preferred_element_type=jnp.float32)  38.6 us
    dot_general x32, matrix products, pair_dot(): jnp.dot(first_pair[1], second_pair[0], preferred_element_type=jnp.float32)  38.5 us
    dot_general x32, matrix products, pair_dot(): jnp.dot(first_pair[0], second_pair[0], preferred_element_type=jnp.float32)  38.3 us
    dot_general x32, matrix products, pair_dot(): jnp.dot(first_pair[0], second_pair[1], preferred_element_type=jnp.float32)  38.2 us
    slice x32, local copies, waits for them, and re-layouts, block_step(): v_weights = kernel_rows(block_offsets[1], block_fractions[1])  26.9 us
    all_to_all x1, waiting for transfers between devices, on_device(): lax.all_to_all(windows, 'facet', split_axis=0, concat_axis=0, tiled=True)  26.6 us
  transfers between devices with their start and end apart: 3, of which 3 were waited for; matrix products, arithmetic and copies ran while one was open for 0% of the time, Pallas kernels for 0%

commit v1 on v0

v1 whole, which is shorter than its diff:
```python
import functools
import math

import jax
import jax.numpy as jnp
import numpy as np
from jax import lax
from jax.experimental import pallas as pl
from jax.experimental.pallas import tpu as pltpu
from jax.sharding import PartitionSpec as P

SUB = 256
MC = 256
STEP = 64
KS = 8
VB = 512
MESH = pl.DeviceIdType.MESH
VMEM = pl.BlockSpec(memory_space=pltpu.VMEM)
SMEM = pl.BlockSpec(memory_space=pltpu.SMEM)
F32 = jnp.float32
BF16 = jnp.bfloat16


def flip(index, bit):
    return index + bit - 2 * bit * ((index // bit) % 2)


def bits_of(count):
    return [1 << level for level in range(count.bit_length() - 1)]


def routes(count):
    bits = bits_of(count)
    return (bits, bits[:1] + bits[:0:-1])


def greet(count):
    me = lax.axis_index("facet")
    barrier = pltpu.get_barrier_semaphore()
    bits = bits_of(count)
    for bit in bits:
        pl.semaphore_signal(
            barrier, inc=1, device_id={"facet": flip(me, bit)}, device_id_type=MESH
        )
    pl.semaphore_wait(barrier, len(bits))


def remote(src, dst, send, recv, axis, target):
    return pltpu.make_async_remote_copy(
        src_ref=src,
        dst_ref=dst,
        send_sem=send,
        recv_sem=recv,
        device_id={axis: target},
        device_id_type=MESH,
    )


def transform_kernel(facets, targets, spec, left_table, right_table, slabs):
    cols = spec.shape[3]

    def transform(slab, carry):
        top = pl.multiple_of(targets[0, slab], STEP)
        left = pl.multiple_of(targets[1, slab], STEP)
        window = jnp.concatenate(
            [spec[0, 0, pl.ds(top, MC), :], spec[0, 1, pl.ds(top, MC), :]], axis=0
        )
        table = right_table[pl.ds(left, cols), :]
        mixed = jnp.dot(window, table, preferred_element_type=F32)
        real = mixed[:MC, :SUB] - mixed[MC:, SUB:]
        imag = mixed[:MC, SUB:] + mixed[MC:, :SUB]
        half = jnp.concatenate([real, imag], axis=0).astype(BF16)
        value = jnp.dot(left_table[...], half, preferred_element_type=F32)
        slabs[slab] = value.astype(BF16).reshape(2, SUB, SUB)
        return carry

    lax.fori_loop(0, facets, transform, 0)


def halve_kernel(facets, slabs, grid_out, total, landed, send, recv):
    me = lax.axis_index("facet")
    greet(facets)
    orders = routes(facets)
    held = [list(range(facets))] * 2
    sent = []
    for level in range(len(orders[0])):
        last = level == len(orders[0]) - 1
        arriving = []
        for part in range(2):
            bit = orders[part][level]
            for slab in reversed([s for s in held[part] if s & bit]):
                source = slabs if level == 0 else total
                copy = remote(
                    source.at[slab, part], landed.at[level, slab - bit, part],
                    send.at[2 * level + part, slab], recv.at[2 * level + part, slab - bit],
                    "facet", flip(me, bit),
                )
                copy.start()
                sent.append(copy)
                arriving.append((copy, slab - bit, part))
            held[part] = [s for s in held[part] if not s & bit]
        for copy, slab, part in arriving:
            copy.wait_recv()
            source = slabs if level == 0 else total
            value = source[slab, part].astype(F32) + landed[level, slab, part].astype(F32)
            if last:
                grid_out[part] = value.astype(BF16)
            else:
                total[slab, part] = value.astype(BF16)
    for copy in sent:
        copy.wait_send()


def kernel_columns(offsets, fractions):
    cells = lax.broadcasted_iota(jnp.int32, (SUB, offsets.shape[1]), 0).astype(F32)
    scale = math.sqrt(math.log2(math.e)) * 9.0 / KS
    centred = cells - (offsets.astype(F32) + (0.5 * KS - 0.5))
    distance = centred * scale - (fractions - 0.5) * scale
    inside = jnp.abs(centred) < 0.5 * KS
    return jnp.where(inside, jnp.exp2(-1.0 - distance * distance), 0.0).astype(BF16)


def vis_kernel(count, grid, offsets, fractions, observed, residual, gridded, flipped, total):
    slots = offsets.shape[2]
    live_count = count[0]
    flipped[:SUB] = grid[0].astype(F32).T.astype(BF16)
    flipped[SUB:] = grid[1].astype(F32).T.astype(BF16)
    total[...] = jnp.zeros_like(total)
    residual[...] = jnp.zeros_like(residual)

    def block(index, carry):
        first = pl.multiple_of(index * VB, VB)
        span = pl.ds(first, VB)
        u_weights = kernel_columns(offsets[0, 0:1, span], fractions[0, 0:1, span])
        v_weights = kernel_columns(offsets[0, 1:2, span], fractions[0, 1:2, span])
        v_float = v_weights.astype(F32)
        product = jnp.dot(flipped[...], u_weights, preferred_element_type=F32)
        live = first + lax.broadcasted_iota(jnp.int32, (1, VB), 1) < live_count
        weighted = []
        for part in range(2):
            model = jnp.sum(product[part * SUB : (part + 1) * SUB] * v_float, axis=0, keepdims=True)
            row = jnp.where(live, observed[0, part : part + 1, span] - model, 0.0)
            residual[0, part : part + 1, span] = row
            weighted.append((row * v_float).astype(BF16))
        total[...] += lax.dot_general(
            u_weights,
            jnp.concatenate(weighted, axis=0),
            (((1,), (1,)), ((), ())),
            preferred_element_type=F32,
        )
        return carry

    lax.fori_loop(0, (live_count + VB - 1) // VB, block, 0)
    gridded[0] = total[:, :SUB].astype(BF16)
    gridded[1] = total[:, SUB:].astype(BF16)


def gather_kernel(facets, own, everyone, slabs, send, recv):
    me = lax.axis_index("facet")
    greet(facets)
    slabs[0] = own[...]
    orders = [order[:0:-1] + order[:1] for order in routes(facets)]
    held = [[0], [0]]
    sent = []
    for level in range(len(orders[0])):
        arriving = []
        for part in range(2):
            bit = orders[part][level]
            for slab in held[part]:
                copy = remote(
                    slabs.at[slab, part], slabs.at[slab + bit, part],
                    send.at[part, slab + bit], recv.at[part, slab + bit],
                    "facet", flip(me, bit),
                )
                copy.start()
                arriving.append(copy)
            held[part] = held[part] + [s + bit for s in held[part]]
        for copy in arriving:
            copy.wait_recv()
        sent += arriving
    everyone[...] = slabs[...]
    for copy in sent:
        copy.wait_send()


def adjoint_kernel(facets, targets, everyone, left_table, right_table, pieces, plane):
    cols = plane.shape[2]
    chunk = pieces.shape[2]
    plane[...] = jnp.zeros_like(plane)

    def add_source(slab, carry):
        top = pl.multiple_of(targets[0, slab], STEP)
        left = pl.multiple_of(targets[1, slab], STEP)
        source = everyone[slab].reshape(2 * SUB, SUB)
        half = jnp.dot(left_table[...], source, preferred_element_type=F32)
        real = half[:MC]
        imag = half[MC:]
        stacked = jnp.concatenate(
            [jnp.concatenate([real, imag], axis=1), jnp.concatenate([imag, -real], axis=1)], axis=0
        ).astype(BF16)
        table = right_table[pl.ds(left, cols), :]
        window = lax.dot_general(
            stacked, table, (((1,), (1,)), ((), ())), preferred_element_type=F32
        )
        plane[0, pl.ds(top, MC), :] += window[:MC]
        plane[1, pl.ds(top, MC), :] += window[MC:]
        return carry

    lax.fori_loop(0, facets, add_source, 0)
    for piece in range(pieces.shape[0]):
        pieces[piece] = plane[:, piece * chunk : (piece + 1) * chunk, :].astype(BF16)


def spread_kernel(groups, pieces, update, landed, send, recv):
    me = lax.axis_index("sub")
    barrier = pltpu.get_barrier_semaphore()
    for hop in range(1, groups):
        pl.semaphore_signal(
            barrier, inc=1, device_id={"sub": (me + hop) % groups}, device_id_type=MESH
        )
    pl.semaphore_wait(barrier, groups - 1)
    copies = []
    for hop in range(1, groups):
        to = (me + hop) % groups
        copy = remote(
            pieces.at[to], landed.at[hop - 1], send.at[hop - 1], recv.at[hop - 1], "sub", to
        )
        copy.start()
        copies.append(copy)
    value = pieces[me].astype(F32)
    for hop, copy in enumerate(copies):
        copy.wait_recv()
        value = value + landed[hop].astype(F32)
    update[0] = value
    for copy in copies:
        copy.wait_send()


def phases(facets):
    modulus = SUB * facets
    centred = np.arange(SUB) - SUB // 2
    base = np.exp(2j * np.pi * (np.outer(centred, centred) * facets % modulus) / modulus)
    turn = np.exp(2j * np.pi * (np.outer(np.arange(facets), centred) % modulus) / modulus)
    pair = lambda z: jnp.asarray(np.stack([z.real, z.imag]).astype(np.float32))
    return pair(base * MC ** (-0.5)), pair(turn)


def turned(base, turn):
    return (base[0] * turn[0] - base[1] * turn[1], base[0] * turn[1] + base[1] * turn[0])


def on_device(facet_spec, worker_of_subgrid, vis_count, bin_offsets, bin_fractions, observed):
    facets = lax.axis_size("facet")
    pos_v = lax.axis_size("sub")
    me = lax.axis_index("facet")
    sub_rank = lax.axis_index("sub")
    rows = facet_spec.shape[2]
    cols = facet_spec.shape[3]
    pad = (pos_v - 1) * STEP
    slots = bin_offsets.shape[2]

    wanted = jnp.bitwise_xor(jnp.arange(facets, dtype=jnp.int32), me) * pos_v + sub_rank
    ids = jnp.arange(worker_of_subgrid.shape[0], dtype=jnp.int32)
    targets = jnp.sum(
        jnp.where(worker_of_subgrid[None, :] == wanted[:, None], ids[None, :], 0), axis=1
    ).astype(jnp.int32)
    targets = jnp.stack([targets // pos_v * STEP, pad - targets % pos_v * STEP])

    base, turn = phases(facets)
    turn_u = lax.dynamic_index_in_dim(turn, me, 1, keepdims=False)
    turn_v = lax.dynamic_index_in_dim(turn, (5 * me + 3) % facets, 1, keepdims=False)
    qa = turned(base, turn_u[:, :, None])
    qa_t = turned(base, turn_u[:, None, :])
    qb_t = turned(base, turn_v[:, None, :])
    join = lambda a, b, c, d: jnp.concatenate(
        [jnp.concatenate([a, b], 1), jnp.concatenate([c, d], 1)], 0
    ).astype(BF16)
    left = join(qa[0], -qa[1], qa[1], qa[0])
    left_adjoint = join(qa_t[0], qa_t[1], -qa_t[1], qa_t[0])
    right = jnp.pad(jnp.concatenate(qb_t, 1).astype(BF16), ((pad, pad), (0, 0)))

    levels = len(bits_of(facets))
    slab_shape = (2, SUB, SUB)
    limit = 60 * 1024 * 1024
    slabs = pl.pallas_call(
        functools.partial(transform_kernel, facets),
        out_shape=jax.ShapeDtypeStruct((facets,) + slab_shape, BF16),
        in_specs=[SMEM, VMEM, VMEM, VMEM],
        out_specs=VMEM,
        compiler_params=pltpu.CompilerParams(vmem_limit_bytes=limit),
        name="transform",
    )(targets, facet_spec, left, right)

    grid = pl.pallas_call(
        functools.partial(halve_kernel, facets),
        out_shape=jax.ShapeDtypeStruct(slab_shape, BF16),
        in_specs=[VMEM],
        out_specs=VMEM,
        scratch_shapes=[
            pltpu.VMEM((facets,) + slab_shape, BF16),
            pltpu.VMEM((levels, facets) + slab_shape, BF16),
            pltpu.SemaphoreType.DMA((2 * levels, facets)),
            pltpu.SemaphoreType.DMA((2 * levels, facets)),
        ],
        compiler_params=pltpu.CompilerParams(
            collective_id=0, has_side_effects=True, vmem_limit_bytes=limit
        ),
        name="sum_grids",
    )(slabs)

    residual, gridded = pl.pallas_call(
        vis_kernel,
        out_shape=(
            jax.ShapeDtypeStruct((1, 2, slots), F32),
            jax.ShapeDtypeStruct(slab_shape, BF16),
        ),
        in_specs=[SMEM, VMEM, VMEM, VMEM, VMEM],
        out_specs=(VMEM, VMEM),
        scratch_shapes=[
            pltpu.VMEM((2 * SUB, SUB), BF16),
            pltpu.VMEM((SUB, 2 * SUB), F32),
        ],
        compiler_params=pltpu.CompilerParams(vmem_limit_bytes=limit),
        name="visibilities",
    )(vis_count, grid, bin_offsets, bin_fractions, observed)

    everyone = pl.pallas_call(
        functools.partial(gather_kernel, facets),
        out_shape=jax.ShapeDtypeStruct((facets,) + slab_shape, BF16),
        in_specs=[VMEM],
        out_specs=VMEM,
        scratch_shapes=[
            pltpu.VMEM((facets,) + slab_shape, BF16),
            pltpu.SemaphoreType.DMA((2, facets)),
            pltpu.SemaphoreType.DMA((2, facets)),
        ],
        compiler_params=pltpu.CompilerParams(
            collective_id=1, has_side_effects=True, vmem_limit_bytes=limit
        ),
        name="gather_grids",
    )(gridded)

    chunk = rows // pos_v
    pieces = pl.pallas_call(
        functools.partial(adjoint_kernel, facets),
        out_shape=jax.ShapeDtypeStruct((pos_v, 2, chunk, cols), BF16),
        in_specs=[SMEM, VMEM, VMEM, VMEM],
        out_specs=VMEM,
        scratch_shapes=[pltpu.VMEM((2, rows, cols), F32)],
        compiler_params=pltpu.CompilerParams(vmem_limit_bytes=limit),
        name="adjoint",
    )(targets, everyone, left_adjoint, right)

    update = pl.pallas_call(
        functools.partial(spread_kernel, pos_v),
        out_shape=jax.ShapeDtypeStruct((1, 2, chunk, cols), F32),
        in_specs=[VMEM],
        out_specs=VMEM,
        scratch_shapes=[
            pltpu.VMEM((pos_v - 1, 2, chunk, cols), BF16),
            pltpu.SemaphoreType.DMA((pos_v - 1,)),
            pltpu.SemaphoreType.DMA((pos_v - 1,)),
        ],
        compiler_params=pltpu.CompilerParams(
            collective_id=2, has_side_effects=True, vmem_limit_bytes=limit
        ),
        name="sum_pieces",
    )(pieces)
    return (residual, update)


def solution(mesh):
    placed = (
        P("facet", None, None, None),
        P(),
        P(("facet", "sub")),
        P(("facet", "sub"), None, None),
        P(("facet", "sub"), None, None),
        P(("facet", "sub"), None, None),
    )
    return jax.shard_map(
        on_device,
        mesh=mesh,
        in_specs=placed,
        out_specs=(P(("facet", "sub"), None, None), P("facet", None, "sub", None)),
        check_vma=False,
    )
```

time: 546 us -> 117 us (0.21)
  matrix products: 168 us -> 0 us
  local copies, waits for them, and re-layouts: 140 us -> 4.32 us
  Pallas kernels: 0 us -> 106 us
  waiting for transfers between devices: 105 us -> 0 us
  other arithmetic: 71.4 us -> 3.99 us
  loops' own time: 31.8 us -> 0 us
  between operations: 14.9 us -> 1.34 us
  starting transfers between devices: 8.11 us -> 0 us
    dot_general x160 -> x0, matrix products: 168 us -> none  [the longest x32 38.6 us: pair_dot(): jnp.dot(first_pair[1], second_pair[1], preferred_element_type=jnp.float32)]
    pallas_call x0 -> x6, Pallas kernels: none -> 106 us  [the longest x1 38 us: on_device(): pl.pallas_call(functools.partial(spread_kernel, pos_v), out_shape=jax.Sha...]
    dynamic_update_slice x8 -> x0, local copies, waits for them, and re-layouts: 69.5 us -> none  [add_window(): lax.dynamic_update_slice(plane, current + window.astype(jnp.float32), (an...]
    reduce_scatter x1 -> x0, waiting for transfers between devices: 53 us -> none  [on_device(): update = lax.psum_scatter(plane, 'sub', scatter_dimension=1, tiled=True)]
    all_to_all x2 -> x0, waiting for transfers between devices: 52.5 us -> none  [the longest x1 26.6 us: on_device(): lax.all_to_all(windows, 'facet', split_axis=0, concat_axis=0, tiled=True)]
    select_n x34 -> x0, other arithmetic: 34.2 us -> none  [the longest x16 23.8 us: block_step(): real_part = jnp.where(live_mask, block_observed[0] - model_real, 0.0)]
    another operation x5 -> x0, loops' own time: 31.8 us -> none  [the longest x1 19.9 us: on_device(): plane = lax.fori_loop(0, pos_u, place_one, plane)]
    slice x32 -> x1, local copies, waits for them, and re-layouts: 26.9 us -> 0.79 us  [turned(): turn[0]]
  transfers between devices with their start and end apart: 3 -> 0, of which waited for: 3 -> 0; matrix products, arithmetic and copies ran while one was open for 0% -> 0% of each run, Pallas kernels for 0% -> 0%
where the time goes in v1:
time: 117 us; the launch traced here: 116 us
  Pallas kernels  106 us (91%)
  local copies, waits for them, and re-layouts  4.32 us (4%)
  other arithmetic  3.99 us (3%)
  between operations  1.34 us (1%)
    pallas_call x1, Pallas kernels, on_device(): pl.pallas_call(functools.partial(spread_kernel, pos_v), out_shape=jax.Sha...  38 us
    pallas_call x1, Pallas kernels, on_device(): pl.pallas_call(functools.partial(gather_kernel, facets), out_shape=jax.Sh...  22.9 us
    pallas_call x1, Pallas kernels, on_device(): pl.pallas_call(functools.partial(halve_kernel, facets), out_shape=jax.Sha...  19.7 us
    pallas_call x1, Pallas kernels, on_device(): pl.pallas_call(functools.partial(transform_kernel, facets), out_shape=jax...  10.7 us
    pallas_call x1, Pallas kernels, on_device(): pl.pallas_call(functools.partial(adjoint_kernel, facets), out_shape=jax.S...  7.97 us
    pallas_call x1, Pallas kernels, on_device(): pl.pallas_call(vis_kernel, out_shape=(jax.ShapeDtypeStruct((1, 2, slots),...  6.86 us
    unnamed x6, local copies, waits for them, and re-layouts  3.53 us

profile of v1, /device:TPU:8, one launch (start us, length us, event | category | flops | bytes accessed | tf_op | source)
XLA Modules:
  0.0 115.8 jit_solution(6579269696630940245)
XLA Ops:
  0.6 0.8 constant_dynamic-slice_fusion.3
  1.4 1.3 %fusion.4 = (bf16[256,256]{1,0:T(8,128)(2,1)S(1)}, bf16[256,256]{1,0:T(8,128)(2,1)S(1)}, bf16[256,256]{1,0:T(8,128)(2,1)S(1)}, bf16[256,256]{1,0:T(8,128)(2,1)S(...) fusion(f32[256,256]{1,0:T(8,128)} %constant.82, ...), kind=kLoop, calls=%fused_computation.10 | loop fusion | flops 1835008 | bytes 1576960 | tf_op jit(solution)/shard_map/convert.5
  2.7 0.0 copy-start.1
  2.7 0.0 copy-start
  2.7 0.9 fusion.3.right_table
  3.6 1.1 maximum_maximum_fusion
  4.7 0.0 copy-done.1
  4.7 0.2 select_reduce_fusion
  4.9 0.6 pad_add_fusion.targets
  5.5 0.0 copy-done
  5.5 1.5 %copy.11.spec = bf16[1,2,704,448]{3,2,1,0:T(8,128)(2,1)} copy(bf16[1,2,704,448]{2,3,1,0:T(8,128)(2,1)S(1)} %copy-done) | data formatting | bytes 2523136 | tf_op args[0]
  7.0 10.7 %transform.1.slabs = bf16[8,2,256,256]{3,2,1,0:T(8,128)(2,1)} custom-call(s32[2,8]{1,0:T(2,128)} %pad_add_fusion.targets, bf16[1,2,704,448]{3,2,1,0:T(8,128)(2,1)} %copy.11.spec, bf16[512,512]{1,0:T(8,128)(2,1)} %get-tuple-element.22.left_table, bf16[640,512]{1,0:T(8,128)(2,1)} %fusion.3.right_table), custom_call_target="tpu_custom_call" | custom-call | tf_op jit(solution)/shard_map/transform/pallas_call | solution.py:285
  17.7 19.7 %sum_grids.1.grid = bf16[2,256,256]{2,1,0:T(8,128)(2,1)} custom-call(bf16[8,2,256,256]{3,2,1,0:T(8,128)(2,1)} %transform.1.slabs), custom_call_target="tpu_custom_call" | custom-call | tf_op jit(solution)/shard_map/sum_grids/pallas_call | solution.py:294
  38.0 6.9 %visibilities.1 = (f32[1,2,8192]{2,1,0:T(2,128)}, bf16[2,256,256]{2,1,0:T(8,128)(2,1)}) custom-call(s32[1]{0:T(128)S(6)} %copy.13.count, bf16[2,256,256]{2,1,0:T(8,128)(2,1)} %sum_grids.1.grid, s32[1,2,8192]{2,1,0:T(2,128)} %offsets.1, f32[1,2,8192]{2,1,0:T(2,128)} %fractions.1, f32[1,2,8192]{2,1,0:T(2,128)} %observed.1), custom_call_target="tpu_custom_call" | custom-call | tf_op jit(solution)/shard_map/visibilities/pallas_call | solution.py:311
  44.8 22.9 %gather_grids.1.everyone = bf16[8,2,256,256]{3,2,1,0:T(8,128)(2,1)} custom-call(bf16[2,256,256]{2,1,0:T(8,128)(2,1)} %get-tuple-element.5.own), custom_call_target="tpu_custom_call" | custom-call | tf_op jit(solution)/shard_map/gather_grids/pallas_call | solution.py:327
  67.8 8.0 %adjoint.1.pieces = bf16[4,2,176,448]{3,2,1,0:T(8,128)(2,1)} custom-call(s32[2,8]{1,0:T(2,128)} %pad_add_fusion.targets, bf16[8,2,256,256]{3,2,1,0:T(8,128)(2,1)} %gather_grids.1.everyone, bf16[512,512]{1,0:T(8,128)(2,1)} %get-tuple-element.23.left_table, bf16[640,512]{1,0:T(8,128)(2,1)} %fusion.3.right_table), custom_call_target="tpu_custom_call" | custom-call | tf_op jit(solution)/shard_map/adjoint/pallas_call | solution.py:344
  75.8 38.0 %sum_pieces.1 = f32[1,2,176,448]{3,2,1,0:T(8,128)} custom-call(bf16[4,2,176,448]{3,2,1,0:T(8,128)(2,1)} %adjoint.1.pieces), custom_call_target="tpu_custom_call" | custom-call | tf_op jit(solution)/shard_map/sum_pieces/pallas_call | solution.py:354
  113.8 2.0 %copy.14 = f32[1,2,176,448]{3,2,1,0:T(8,128)} copy(f32[1,2,176,448]{3,2,1,0:T(8,128)} %sum_pieces.1) | data formatting | bytes 1261568
  (2 shorter events, 0.0 us)
Async XLA Ops:
  2.7 2.0 %copy-start.1 = (s32[32]{0:T(128)S(1)}, s32[32]{0:T(128)}, u32[]{:S(2)}) copy-start(s32[32]{0:T(128)} %param.9) | copy-start | bytes 388
  2.7 2.8 %copy-start = (bf16[1,2,704,448]{2,3,1,0:T(8,128)(2,1)S(1)}, bf16[1,2,704,448]{2,3,1,0:T(8,128)(2,1)}, u32[]{:S(2)}) copy-start(bf16[1,2,704,448]{2,3,1,0:T(8,128)(2,1)} %param.8) | copy-start | bytes 3784708

commit v2 on v1

--- a/solution.py
+++ b/solution.py
@@ -56,12 +56,51 @@
     )
 
 
-def transform_kernel(facets, targets, spec, left_table, right_table, slabs):
+def transform_kernel(
+    facets, pos_v, base, turns, worker, spec, slabs, left_adjoint, right_table, corners, left_table, holder
+):
     cols = spec.shape[3]
+    pad = (pos_v - 1) * STEP
+    me = lax.axis_index("facet")
+    rank = lax.axis_index("sub")
+
+    def note(subgrid, carry):
+        holder[worker[subgrid]] = subgrid
+        return carry
+
+    lax.fori_loop(0, worker.shape[0], note, 0)
+    for slab in range(facets):
+        member = me
+        for bit in bits_of(facets):
+            member = flip(member, bit) if slab & bit else member
+        subgrid = holder[member * pos_v + rank]
+        corners[0, slab] = subgrid // pos_v * STEP
+        corners[1, slab] = pad - subgrid % pos_v * STEP
+
+    def turned(facet):
+        turn = turns[facet]
+        real, imag = turn[0:1], turn[1:2]
+        return (base[0] * real - base[1] * imag, base[0] * imag + base[1] * real)
+
+    real, imag = turned(me)
+    left_adjoint[:MC, :SUB] = real.astype(BF16)
+    left_adjoint[:MC, SUB:] = imag.astype(BF16)
+    left_adjoint[MC:, :SUB] = (-imag).astype(BF16)
+    left_adjoint[MC:, SUB:] = real.astype(BF16)
+    real, imag = real.T, imag.T
+    left_table[:SUB, :MC] = real.astype(BF16)
+    left_table[:SUB, MC:] = (-imag).astype(BF16)
+    left_table[SUB:, :MC] = imag.astype(BF16)
+    left_table[SUB:, MC:] = real.astype(BF16)
+    real, imag = turned((5 * me + 3) % facets)
+    right_table[:pad] = jnp.zeros((pad, 2 * SUB), BF16)
+    right_table[pad + MC :] = jnp.zeros((pad, 2 * SUB), BF16)
+    right_table[pad : pad + MC, :SUB] = real.astype(BF16)
+    right_table[pad : pad + MC, SUB:] = imag.astype(BF16)
 
     def transform(slab, carry):
-        top = pl.multiple_of(targets[0, slab], STEP)
-        left = pl.multiple_of(targets[1, slab], STEP)
+        top = pl.multiple_of(corners[0, slab], STEP)
+        left = pl.multiple_of(corners[1, slab], STEP)
         window = jnp.concatenate(
             [spec[0, 0, pl.ds(top, MC), :], spec[0, 1, pl.ds(top, MC), :]], axis=0
         )
@@ -74,39 +113,52 @@
         slabs[slab] = value.astype(BF16).reshape(2, SUB, SUB)
         return carry
 
-    lax.fori_loop(0, facets, transform, 0)
+    lax.fori_loop(0, facets, transform, 0, unroll=2)
 
 
 def halve_kernel(facets, slabs, grid_out, total, landed, send, recv):
     me = lax.axis_index("facet")
     greet(facets)
     orders = routes(facets)
+    levels = len(orders[0])
+    sent = []
+
+    def queue(part, level, held):
+        rank = lambda slab: tuple(not slab & bit for bit in orders[part][level:])
+        return sorted(held, key=rank)
+
+    def copy_of(source, level, slab, part):
+        bit = orders[part][level]
+        return remote(
+            source.at[slab, part], landed.at[level, slab - bit, part],
+            send.at[2 * level + part, slab], recv.at[2 * level + part, slab - bit],
+            "facet", flip(me, bit),
+        )
+
+    def post(source, level, slab, part):
+        copy = copy_of(source, level, slab, part)
+        copy.start()
+        sent.append(copy)
+
     held = [list(range(facets))] * 2
-    sent = []
-    for level in range(len(orders[0])):
-        last = level == len(orders[0]) - 1
-        arriving = []
-        for part in range(2):
-            bit = orders[part][level]
-            for slab in reversed([s for s in held[part] if s & bit]):
+    pairs = [queue(part, 0, [s for s in held[part] if s & 1]) for part in range(2)]
+    for both in zip(*pairs):
+        for part, slab in enumerate(both):
+            post(slabs, 0, slab, part)
+    for level in range(levels):
+        held = [[s for s in held[p] if not s & orders[p][level]] for p in range(2)]
+        pairs = [queue(part, level + 1, held[part]) for part in range(2)]
+        for both in zip(*pairs):
+            for part, slab in enumerate(both):
+                copy_of(slabs, level, slab + orders[part][level], part).wait_recv()
                 source = slabs if level == 0 else total
-                copy = remote(
-                    source.at[slab, part], landed.at[level, slab - bit, part],
-                    send.at[2 * level + part, slab], recv.at[2 * level + part, slab - bit],
-                    "facet", flip(me, bit),
-                )
-                copy.start()
-                sent.append(copy)
-                arriving.append((copy, slab - bit, part))
-            held[part] = [s for s in held[part] if not s & bit]
-        for copy, slab, part in arriving:
-            copy.wait_recv()
-            source = slabs if level == 0 else total
-            value = source[slab, part].astype(F32) + landed[level, slab, part].astype(F32)
-            if last:
-                grid_out[part] = value.astype(BF16)
-            else:
-                total[slab, part] = value.astype(BF16)
+                value = source[slab, part].astype(F32) + landed[level, slab, part].astype(F32)
+                if level == levels - 1:
+                    grid_out[part] = value.astype(BF16)
+                else:
+                    total[slab, part] = value.astype(BF16)
+                    if slab & orders[part][level + 1]:
+                        post(total, level + 1, slab, part)
     for copy in sent:
         copy.wait_send()
 
@@ -155,30 +207,39 @@
     gridded[1] = total[:, SUB:].astype(BF16)
 
 
-def gather_kernel(facets, own, everyone, slabs, send, recv):
+def gather_kernel(facets, own, slabs, send, recv):
     me = lax.axis_index("facet")
     greet(facets)
+    orders = [order[:0:-1] + order[:1] for order in routes(facets)]
+    levels = len(orders[0])
+    sent = []
+
+    def copy_of(level, slab, part):
+        bit = orders[part][level]
+        source = slabs.at[slab, part] if slab else own.at[part]
+        return remote(
+            source, slabs.at[slab + bit, part],
+            send.at[part, slab + bit], recv.at[part, slab + bit],
+            "facet", flip(me, bit),
+        )
+
+    def post(level, slab, part):
+        copy = copy_of(level, slab, part)
+        copy.start()
+        sent.append(copy)
+
+    for level in range(levels):
+        for part in range(2):
+            post(level, 0, part)
     slabs[0] = own[...]
-    orders = [order[:0:-1] + order[:1] for order in routes(facets)]
     held = [[0], [0]]
-    sent = []
-    for level in range(len(orders[0])):
-        arriving = []
-        for part in range(2):
-            bit = orders[part][level]
-            for slab in held[part]:
-                copy = remote(
-                    slabs.at[slab, part], slabs.at[slab + bit, part],
-                    send.at[part, slab + bit], recv.at[part, slab + bit],
-                    "facet", flip(me, bit),
-                )
-                copy.start()
-                arriving.append(copy)
-            held[part] = held[part] + [s + bit for s in held[part]]
-        for copy in arriving:
-            copy.wait_recv()
-        sent += arriving
-    everyone[...] = slabs[...]
+    for level in range(levels):
+        for both in zip(*held):
+            for part, slab in enumerate(both):
+                copy_of(level, slab, part).wait_recv()
+                for later in range(level + 1, levels):
+                    post(later, slab + orders[part][level], part)
+        held = [held[p] + [s + orders[p][level] for s in held[p]] for p in range(2)]
     for copy in sent:
         copy.wait_send()
 
@@ -206,34 +267,74 @@
         plane[1, pl.ds(top, MC), :] += window[MC:]
         return carry
 
-    lax.fori_loop(0, facets, add_source, 0)
+    lax.fori_loop(0, facets, add_source, 0, unroll=2)
     for piece in range(pieces.shape[0]):
         pieces[piece] = plane[:, piece * chunk : (piece + 1) * chunk, :].astype(BF16)
 
 
-def spread_kernel(groups, pieces, update, landed, send, recv):
+def line_kernel(groups, pieces, update, totals, landed, send, recv):
     me = lax.axis_index("sub")
     barrier = pltpu.get_barrier_semaphore()
-    for hop in range(1, groups):
-        pl.semaphore_signal(
-            barrier, inc=1, device_id={"sub": (me + hop) % groups}, device_id_type=MESH
-        )
-    pl.semaphore_wait(barrier, groups - 1)
-    copies = []
-    for hop in range(1, groups):
-        to = (me + hop) % groups
-        copy = remote(
-            pieces.at[to], landed.at[hop - 1], send.at[hop - 1], recv.at[hop - 1], "sub", to
-        )
-        copy.start()
-        copies.append(copy)
-    value = pieces[me].astype(F32)
-    for hop, copy in enumerate(copies):
-        copy.wait_recv()
-        value = value + landed[hop].astype(F32)
-    update[0] = value
-    for copy in copies:
-        copy.wait_send()
+    inner = (me > 0, me < groups - 1)
+    ends = (me == 0, me == groups - 1)
+    ahead = ((me + 1) % groups, (me + groups - 1) % groups)
+    behind = (ahead[1], ahead[0])
+    for way in range(2):
+        @pl.when(inner[way])
+        def _():
+            pl.semaphore_signal(
+                barrier, inc=1, device_id={"sub": behind[way]}, device_id_type=MESH
+            )
+    between = jnp.logical_and(inner[0], inner[1])
+
+    @pl.when(between)
+    def _():
+        pl.semaphore_wait(barrier, 2)
+
+    @pl.when(jnp.logical_not(between))
+    def _():
+        pl.semaphore_wait(barrier, 1)
+
+    def copy_of(source, way, chunk, part):
+        return remote(
+            source, landed.at[way, chunk, part],
+            send.at[way, chunk, part], recv.at[way, chunk, part], "sub", ahead[way],
+        )
+
+    def sends(way, chunk):
+        return me < chunk if way == 0 else me > chunk
+
+    steps = [
+        (way, chunk if way == 0 else groups - 1 - chunk, part)
+        for chunk in range(groups - 1, 0, -1)
+        for part in range(2)
+        for way in range(2)
+    ]
+    for way, chunk, part in steps:
+        @pl.when(ends[way])
+        def _():
+            copy_of(pieces.at[chunk, part], way, chunk, part).start()
+
+        @pl.when(jnp.logical_and(inner[way], sends(way, chunk)))
+        def _():
+            copy_of(pieces.at[chunk, part], way, chunk, part).wait_recv()
+            totals[way, chunk, part] = (
+                pieces[chunk, part].astype(F32) + landed[way, chunk, part].astype(F32)
+            ).astype(BF16)
+            copy_of(totals.at[way, chunk, part], way, chunk, part).start()
+
+    for part in range(2):
+        update[0, part] = pieces[me, part].astype(F32)
+    for part in range(2):
+        for way in range(2):
+            @pl.when(inner[way])
+            def _():
+                copy_of(pieces.at[me, part], way, me, part).wait_recv()
+                update[0, part] += landed[way, me, part].astype(F32)
+    for way, chunk, part in steps:
+        @pl.when(sends(way, chunk))
+        def _():
+            copy_of(pieces.at[chunk, part], way, chunk, part).wait_send()
 
 
 def phases(facets):
@@ -242,54 +343,37 @@
     base = np.exp(2j * np.pi * (np.outer(centred, centred) * facets % modulus) / modulus)
     turn = np.exp(2j * np.pi * (np.outer(np.arange(facets), centred) % modulus) / modulus)
     pair = lambda z: jnp.asarray(np.stack([z.real, z.imag]).astype(np.float32))
-    return pair(base * MC ** (-0.5)), pair(turn)
-
-
-def turned(base, turn):
-    return (base[0] * turn[0] - base[1] * turn[1], base[0] * turn[1] + base[1] * turn[0])
+    return pair(base * MC ** (-0.5)), jnp.swapaxes(pair(turn), 0, 1)
 
 
 def on_device(facet_spec, worker_of_subgrid, vis_count, bin_offsets, bin_fractions, observed):
     facets = lax.axis_size("facet")
     pos_v = lax.axis_size("sub")
-    me = lax.axis_index("facet")
-    sub_rank = lax.axis_index("sub")
     rows = facet_spec.shape[2]
     cols = facet_spec.shape[3]
     pad = (pos_v - 1) * STEP
     slots = bin_offsets.shape[2]
-
-    wanted = jnp.bitwise_xor(jnp.arange(facets, dtype=jnp.int32), me) * pos_v + sub_rank
-    ids = jnp.arange(worker_of_subgrid.shape[0], dtype=jnp.int32)
-    targets = jnp.sum(
-        jnp.where(worker_of_subgrid[None, :] == wanted[:, None], ids[None, :], 0), axis=1
-    ).astype(jnp.int32)
-    targets = jnp.stack([targets // pos_v * STEP, pad - targets % pos_v * STEP])
-
-    base, turn = phases(facets)
-    turn_u = lax.dynamic_index_in_dim(turn, me, 1, keepdims=False)
-    turn_v = lax.dynamic_index_in_dim(turn, (5 * me + 3) % facets, 1, keepdims=False)
-    qa = turned(base, turn_u[:, :, None])
-    qa_t = turned(base, turn_u[:, None, :])
-    qb_t = turned(base, turn_v[:, None, :])
-    join = lambda a, b, c, d: jnp.concatenate(
-        [jnp.concatenate([a, b], 1), jnp.concatenate([c, d], 1)], 0
-    ).astype(BF16)
-    left = join(qa[0], -qa[1], qa[1], qa[0])
-    left_adjoint = join(qa_t[0], qa_t[1], -qa_t[1], qa_t[0])
-    right = jnp.pad(jnp.concatenate(qb_t, 1).astype(BF16), ((pad, pad), (0, 0)))
-
+    base, turns = phases(facets)
     levels = len(bits_of(facets))
     slab_shape = (2, SUB, SUB)
     limit = 60 * 1024 * 1024
-    slabs = pl.pallas_call(
-        functools.partial(transform_kernel, facets),
-        out_shape=jax.ShapeDtypeStruct((facets,) + slab_shape, BF16),
-        in_specs=[SMEM, VMEM, VMEM, VMEM],
-        out_specs=VMEM,
+    slabs, left_adjoint, right, corners = pl.pallas_call(
+        functools.partial(transform_kernel, facets, pos_v),
+        out_shape=(
+            jax.ShapeDtypeStruct((facets,) + slab_shape, BF16),
+            jax.ShapeDtypeStruct((2 * MC, 2 * SUB), BF16),
+            jax.ShapeDtypeStruct((MC + 2 * pad, 2 * SUB), BF16),
+            jax.ShapeDtypeStruct((2, facets), jnp.int32),
+        ),
+        in_specs=[VMEM, VMEM, SMEM, VMEM],
+        out_specs=(VMEM, VMEM, VMEM, SMEM),
+        scratch_shapes=[
+            pltpu.VMEM((2 * SUB, 2 * MC), BF16),
+            pltpu.SMEM(worker_of_subgrid.shape, jnp.int32),
+        ],
         compiler_params=pltpu.CompilerParams(vmem_limit_bytes=limit),
         name="transform",
-    )(targets, facet_spec, left, right)
+    )(base, turns, worker_of_subgrid, facet_spec)
 
     grid = pl.pallas_call(
         functools.partial(halve_kernel, facets),
@@ -330,7 +414,6 @@
         in_specs=[VMEM],
         out_specs=VMEM,
         scratch_shapes=[
-            pltpu.VMEM((facets,) + slab_shape, BF16),
             pltpu.SemaphoreType.DMA((2, facets)),
             pltpu.SemaphoreType.DMA((2, facets)),
         ],
@@ -349,17 +432,18 @@
         scratch_shapes=[pltpu.VMEM((2, rows, cols), F32)],
         compiler_params=pltpu.CompilerParams(vmem_limit_bytes=limit),
         name="adjoint",
-    )(targets, everyone, left_adjoint, right)
+    )(corners, everyone, left_adjoint, right)
 
     update = pl.pallas_call(
-        functools.partial(spread_kernel, pos_v),
+        functools.partial(line_kernel, pos_v),
         out_shape=jax.ShapeDtypeStruct((1, 2, chunk, cols), F32),
         in_specs=[VMEM],
         out_specs=VMEM,
         scratch_shapes=[
-            pltpu.VMEM((pos_v - 1, 2, chunk, cols), BF16),
-            pltpu.SemaphoreType.DMA((pos_v - 1,)),
-            pltpu.SemaphoreType.DMA((pos_v - 1,)),
+            pltpu.VMEM((2, pos_v, 2, chunk, cols), BF16),
+            pltpu.VMEM((2, pos_v, 2, chunk, cols), BF16),
+            pltpu.SemaphoreType.DMA((2, pos_v, 2)),
+            pltpu.SemaphoreType.DMA((2, pos_v, 2)),
         ],
         compiler_params=pltpu.CompilerParams(
             collective_id=2, has_side_effects=True, vmem_limit_bytes=limit

time: 117 us -> 107 us (0.915); the launches traced: 116 us -> 107 us
  Pallas kernels: 106 us -> 101 us
  other arithmetic: 3.99 us -> 0 us
    pallas_call x1, Pallas kernels: 19.7 us -> 16.6 us  [on_device(): pl.pallas_call(functools.partial(halve_kernel, facets), out_shape=jax.Sha...]
    concatenate x2 -> x0, other arithmetic: 1.94 us -> none  [the longest x1 1.06 us: on_device(): jnp.concatenate([jnp.concatenate([a, b], 1), jnp.concatenate([c, d], 1)], 0)]
    another operation x2 -> x0, other arithmetic: 1.84 us -> none
    pallas_call x2, Pallas kernels: 48.7 us -> 46.9 us  [the longest x1 35.3 us: on_device(): pl.pallas_call(functools.partial(line_kernel, pos_v), out_shape=jax.Shape...]
    unnamed x6 -> x2, local copies, waits for them, and re-layouts: 3.53 us -> 4.52 us
where the time goes in v2:
time: 107 us
  Pallas kernels  101 us (94%)
  local copies, waits for them, and re-layouts  4.52 us (4%)
  between operations  1.31 us (1%)
    pallas_call x1, Pallas kernels, on_device(): pl.pallas_call(functools.partial(line_kernel, pos_v), out_shape=jax.Shape...  35.3 us
    pallas_call x1, Pallas kernels, on_device(): pl.pallas_call(functools.partial(gather_kernel, facets), out_shape=jax.Sh...  23.3 us
    pallas_call x1, Pallas kernels, on_device(): pl.pallas_call(functools.partial(halve_kernel, facets), out_shape=jax.Sha...  16.6 us
    pallas_call x1, Pallas kernels, on_device(): pl.pallas_call(functools.partial(transform_kernel, facets, pos_v), out_sh...  11.6 us
    pallas_call x1, Pallas kernels, on_device(): pl.pallas_call(functools.partial(adjoint_kernel, facets), out_shape=jax.S...  8.27 us
    pallas_call x1, Pallas kernels, on_device(): pl.pallas_call(vis_kernel, out_shape=(jax.ShapeDtypeStruct((1, 2, slots),...  6.04 us
    unnamed x2, local copies, waits for them, and re-layouts  4.52 us

profile of v2, /device:TPU:8, one launch (start us, length us, event | category | flops | bytes accessed | tf_op | source)
XLA Modules:
  0.0 107.0 jit_solution(4028676974034942755)
XLA Ops:
  1.3 2.5 %copy.10.spec = bf16[1,2,704,448]{3,2,1,0:T(8,128)(2,1)} copy(bf16[1,2,704,448]{2,3,1,0:T(8,128)(2,1)} %param.8) | data formatting | bytes 2523136 | tf_op args[0]
  3.8 11.6 %transform.1 = (bf16[8,2,256,256]{3,2,1,0:T(8,128)(2,1)}, bf16[512,512]{1,0:T(8,128)(2,1)}, bf16[640,512]{1,0:T(8,128)(2,1)}, s32[2,8]{1,0:T(2,128)}) custom-call(f32[2,256,256]{2,1,0:T(8,128)} %constant.4.clone.base, f32[8,2,256]{2,1,0:T(2,128)} %constant.11.turns, s32[32]{0:T(128)} %worker.1, bf16[1,2,704,448]{3,2,1,0:T(8,128)(2,1)} %copy.10.spec), custom_call_target="tpu_custom_call" | custom-call | tf_op jit(solution)/shard_map/transform/pallas_call | solution.py:360
  15.4 16.6 %sum_grids.1.grid = bf16[2,256,256]{2,1,0:T(8,128)(2,1)} custom-call(bf16[8,2,256,256]{3,2,1,0:T(8,128)(2,1)} %get-tuple-element.8.slabs), custom_call_target="tpu_custom_call" | custom-call | tf_op jit(solution)/shard_map/sum_grids/pallas_call | solution.py:378
  32.0 6.0 %visibilities.1 = (f32[1,2,8192]{2,1,0:T(2,128)}, bf16[2,256,256]{2,1,0:T(8,128)(2,1)}) custom-call(s32[1]{0:T(128)S(6)} %copy.12.count, bf16[2,256,256]{2,1,0:T(8,128)(2,1)} %sum_grids.1.grid, s32[1,2,8192]{2,1,0:T(2,128)} %offsets.1, f32[1,2,8192]{2,1,0:T(2,128)} %fractions.1, f32[1,2,8192]{2,1,0:T(2,128)} %observed.1), custom_call_target="tpu_custom_call" | custom-call | tf_op jit(solution)/shard_map/visibilities/pallas_call | solution.py:395
  38.1 23.3 %gather_grids.1.everyone = bf16[8,2,256,256]{3,2,1,0:T(8,128)(2,1)} custom-call(bf16[2,256,256]{2,1,0:T(8,128)(2,1)} %get-tuple-element.11.own), custom_call_target="tpu_custom_call" | custom-call | tf_op jit(solution)/shard_map/gather_grids/pallas_call | solution.py:411
  61.4 8.3 %adjoint.1.pieces = bf16[4,2,176,448]{3,2,1,0:T(8,128)(2,1)} custom-call(s32[2,8]{1,0:T(2,128)} %get-tuple-element.10.targets, bf16[8,2,256,256]{3,2,1,0:T(8,128)(2,1)} %gather_grids.1.everyone, bf16[512,512]{1,0:T(8,128)(2,1)} %get-tuple-element.12.left_table, bf16[640,512]{1,0:T(8,128)(2,1)} %get-tuple-element.13.right_table), custom_call_target="tpu_custom_call" | custom-call | tf_op jit(solution)/shard_map/adjoint/pallas_call | solution.py:427
  69.7 35.3 %sum_pieces.1 = f32[1,2,176,448]{3,2,1,0:T(8,128)} custom-call(bf16[4,2,176,448]{3,2,1,0:T(8,128)(2,1)} %adjoint.1.pieces), custom_call_target="tpu_custom_call" | custom-call | tf_op jit(solution)/shard_map/sum_pieces/pallas_call | solution.py:437
  105.0 2.0 %copy.13 = f32[1,2,176,448]{3,2,1,0:T(8,128)} copy(f32[1,2,176,448]{3,2,1,0:T(8,128)} %sum_pieces.1) | data formatting | bytes 1261568

commit v3 on v2

--- a/solution.py
+++ b/solution.py
@@ -57,7 +57,8 @@
 
 
 def transform_kernel(
-    facets, pos_v, base, turns, worker, spec, slabs, left_adjoint, right_table, corners, left_table, holder
+    facets, pos_v, base, turns, worker, spec, slabs, left_adjoint, right_table,
+    turned_table, corners, left_table, holder
 ):
     cols = spec.shape[3]
     pad = (pos_v - 1) * STEP
@@ -93,10 +94,11 @@
     left_table[SUB:, :MC] = imag.astype(BF16)
     left_table[SUB:, MC:] = real.astype(BF16)
     real, imag = turned((5 * me + 3) % facets)
-    right_table[:pad] = jnp.zeros((pad, 2 * SUB), BF16)
-    right_table[pad + MC :] = jnp.zeros((pad, 2 * SUB), BF16)
-    right_table[pad : pad + MC, :SUB] = real.astype(BF16)
-    right_table[pad : pad + MC, SUB:] = imag.astype(BF16)
+    for table, first, second in ((right_table, real, imag), (turned_table, -imag, real)):
+        table[:pad] = jnp.zeros((pad, 2 * SUB), BF16)
+        table[pad + MC :] = jnp.zeros((pad, 2 * SUB), BF16)
+        table[pad : pad + MC, :SUB] = first.astype(BF16)
+        table[pad : pad + MC, SUB:] = second.astype(BF16)
 
     def transform(slab, carry):
         top = pl.multiple_of(corners[0, slab], STEP)
@@ -180,8 +182,7 @@
     total[...] = jnp.zeros_like(total)
     residual[...] = jnp.zeros_like(residual)
 
-    def block(index, carry):
-        first = pl.multiple_of(index * VB, VB)
+    def half_block(first):
         span = pl.ds(first, VB)
         u_weights = kernel_columns(offsets[0, 0:1, span], fractions[0, 0:1, span])
         v_weights = kernel_columns(offsets[0, 1:2, span], fractions[0, 1:2, span])
@@ -194,15 +195,19 @@
             row = jnp.where(live, observed[0, part : part + 1, span] - model, 0.0)
             residual[0, part : part + 1, span] = row
             weighted.append((row * v_float).astype(BF16))
-        total[...] += lax.dot_general(
+        return lax.dot_general(
             u_weights,
             jnp.concatenate(weighted, axis=0),
             (((1,), (1,)), ((), ())),
             preferred_element_type=F32,
         )
+
+    def block(index, carry):
+        first = pl.multiple_of(index * 2 * VB, 2 * VB)
+        total[...] += half_block(first) + half_block(first + VB)
         return carry
 
-    lax.fori_loop(0, (live_count + VB - 1) // VB, block, 0)
+    lax.fori_loop(0, (live_count + 2 * VB - 1) // (2 * VB), block, 0)
     gridded[0] = total[:, :SUB].astype(BF16)
     gridded[1] = total[:, SUB:].astype(BF16)
 
@@ -244,39 +249,33 @@
         copy.wait_send()
 
 
-def adjoint_kernel(facets, targets, everyone, left_table, right_table, pieces, plane):
-    cols = plane.shape[2]
-    chunk = pieces.shape[2]
+def adjoint_kernel(facets, corners, everyone, left_table, right_table, turned_table, pieces, plane):
+    cols = plane.shape[1] // 2
+    chunk = pieces.shape[1]
     plane[...] = jnp.zeros_like(plane)
 
     def add_source(slab, carry):
-        top = pl.multiple_of(targets[0, slab], STEP)
-        left = pl.multiple_of(targets[1, slab], STEP)
+        top = pl.multiple_of(corners[0, slab], STEP)
+        left = pl.multiple_of(corners[1, slab], STEP)
         source = everyone[slab].reshape(2 * SUB, SUB)
         half = jnp.dot(left_table[...], source, preferred_element_type=F32)
-        real = half[:MC]
-        imag = half[MC:]
-        stacked = jnp.concatenate(
-            [jnp.concatenate([real, imag], axis=1), jnp.concatenate([imag, -real], axis=1)], axis=0
-        ).astype(BF16)
-        table = right_table[pl.ds(left, cols), :]
-        window = lax.dot_general(
-            stacked, table, (((1,), (1,)), ((), ())), preferred_element_type=F32
-        )
-        plane[0, pl.ds(top, MC), :] += window[:MC]
-        plane[1, pl.ds(top, MC), :] += window[MC:]
+        row = jnp.concatenate([half[:MC], half[MC:]], axis=1).astype(BF16)
+        table = jnp.concatenate(
+            [right_table[pl.ds(left, cols), :], turned_table[pl.ds(left, cols), :]], axis=0
+        )
+        window = lax.dot_general(row, table, (((1,), (1,)), ((), ())), preferred_element_type=F32)
+        plane[pl.ds(top, MC), :] += window
         return carry
 
     lax.fori_loop(0, facets, add_source, 0, unroll=2)
     for piece in range(pieces.shape[0]):
-        pieces[piece] = plane[:, piece * chunk : (piece + 1) * chunk, :].astype(BF16)
+        pieces[piece] = plane[piece * chunk : (piece + 1) * chunk, :].astype(BF16)
 
 
 def line_kernel(groups, pieces, update, totals, landed, send, recv):
     me = lax.axis_index("sub")
     barrier = pltpu.get_barrier_semaphore()
     inner = (me > 0, me < groups - 1)
-    ends = (me == 0, me == groups - 1)
     ahead = ((me + 1) % groups, (me + groups - 1) % groups)
     behind = (ahead[1], ahead[0])
     for way in range(2):
@@ -295,46 +294,50 @@
     def _():
         pl.semaphore_wait(barrier, 1)
 
+    cols = update.shape[3]
+    size = pieces.shape[1]
+    cut = (size // 2 + 15) // 16 * 16
+    spans = (pl.ds(0, cut), pl.ds(cut, size - cut))
+
     def copy_of(source, way, chunk, part):
         return remote(
-            source, landed.at[way, chunk, part],
+            source.at[chunk, spans[part]], landed.at[way, chunk, spans[part]],
             send.at[way, chunk, part], recv.at[way, chunk, part], "sub", ahead[way],
         )
 
-    def sends(way, chunk):
-        return me < chunk if way == 0 else me > chunk
-
-    steps = [
-        (way, chunk if way == 0 else groups - 1 - chunk, part)
-        for chunk in range(groups - 1, 0, -1)
-        for part in range(2)
-        for way in range(2)
-    ]
-    for way, chunk, part in steps:
-        @pl.when(ends[way])
+    def plan(place):
+        steps = []
+        for way in range(2):
+            depth = place if way == 0 else groups - 1 - place
+            for turn in range(2 * (groups - 1 - depth)):
+                chunk = turn // 2 if way else groups - 1 - turn // 2
+                steps.append((turn + depth, depth, way, chunk, turn % 2))
+        return sorted(steps)
+
+    for place in range(groups):
+        @pl.when(me == place)
         def _():
-            copy_of(pieces.at[chunk, part], way, chunk, part).start()
-
-        @pl.when(jnp.logical_and(inner[way], sends(way, chunk)))
-        def _():
-            copy_of(pieces.at[chunk, part], way, chunk, part).wait_recv()
-            totals[way, chunk, part] = (
-                pieces[chunk, part].astype(F32) + landed[way, chunk, part].astype(F32)
-            ).astype(BF16)
-            copy_of(totals.at[way, chunk, part], way, chunk, part).start()
-
-    for part in range(2):
-        update[0, part] = pieces[me, part].astype(F32)
-    for part in range(2):
-        for way in range(2):
-            @pl.when(inner[way])
-            def _():
-                copy_of(pieces.at[me, part], way, me, part).wait_recv()
-                update[0, part] += landed[way, me, part].astype(F32)
-    for way, chunk, part in steps:
-        @pl.when(sends(way, chunk))
-        def _():
-            copy_of(pieces.at[chunk, part], way, chunk, part).wait_send()
+            for _, depth, way, chunk, part in plan(place):
+                if depth == 0:
+                    copy_of(pieces, way, chunk, part).start()
+                    continue
+                copy_of(pieces, way, chunk, part).wait_recv()
+                totals[way, chunk, spans[part]] = (
+                    pieces[chunk, spans[part]].astype(F32)
+                    + landed[way, chunk, spans[part]].astype(F32)
+                ).astype(BF16)
+                copy_of(totals.at[way], way, chunk, part).start()
+            for part in range(2):
+                span = spans[part]
+                value = pieces[place, span].astype(F32)
+                for way in range(2):
+                    if place != (0, groups - 1)[way]:
+                        copy_of(pieces, way, place, part).wait_recv()
+                        value = value + landed[way, place, span].astype(F32)
+                update[0, 0, span] = value[:, :cols]
+                update[0, 1, span] = value[:, cols:]
+            for _, depth, way, chunk, part in plan(place):
+                copy_of(pieces, way, chunk, part).wait_send()
 
 
 def phases(facets):
@@ -357,16 +360,17 @@
     levels = len(bits_of(facets))
     slab_shape = (2, SUB, SUB)
     limit = 60 * 1024 * 1024
-    slabs, left_adjoint, right, corners = pl.pallas_call(
+    slabs, left_adjoint, right, right_turned, corners = pl.pallas_call(
         functools.partial(transform_kernel, facets, pos_v),
         out_shape=(
             jax.ShapeDtypeStruct((facets,) + slab_shape, BF16),
             jax.ShapeDtypeStruct((2 * MC, 2 * SUB), BF16),
             jax.ShapeDtypeStruct((MC + 2 * pad, 2 * SUB), BF16),
+            jax.ShapeDtypeStruct((MC + 2 * pad, 2 * SUB), BF16),
             jax.ShapeDtypeStruct((2, facets), jnp.int32),
         ),
         in_specs=[VMEM, VMEM, SMEM, VMEM],
-        out_specs=(VMEM, VMEM, VMEM, SMEM),
+        out_specs=(VMEM, VMEM, VMEM, VMEM, SMEM),
         scratch_shapes=[
             pltpu.VMEM((2 * SUB, 2 * MC), BF16),
             pltpu.SMEM(worker_of_subgrid.shape, jnp.int32),
@@ -426,13 +430,13 @@
     chunk = rows // pos_v
     pieces = pl.pallas_call(
         functools.partial(adjoint_kernel, facets),
-        out_shape=jax.ShapeDtypeStruct((pos_v, 2, chunk, cols), BF16),
-        in_specs=[SMEM, VMEM, VMEM, VMEM],
+        out_shape=jax.ShapeDtypeStruct((pos_v, chunk, 2 * cols), BF16),
+        in_specs=[SMEM, VMEM, VMEM, VMEM, VMEM],
         out_specs=VMEM,
-        scratch_shapes=[pltpu.VMEM((2, rows, cols), F32)],
+        scratch_shapes=[pltpu.VMEM((rows, 2 * cols), F32)],
         compiler_params=pltpu.CompilerParams(vmem_limit_bytes=limit),
         name="adjoint",
-    )(corners, everyone, left_adjoint, right)
+    )(corners, everyone, left_adjoint, right, right_turned)
 
     update = pl.pallas_call(
         functools.partial(line_kernel, pos_v),
@@ -440,8 +444,8 @@
         in_specs=[VMEM],
         out_specs=VMEM,
         scratch_shapes=[
-            pltpu.VMEM((2, pos_v, 2, chunk, cols), BF16),
-            pltpu.VMEM((2, pos_v, 2, chunk, cols), BF16),
+            pltpu.VMEM((2, pos_v, chunk, 2 * cols), BF16),
+            pltpu.VMEM((2, pos_v, chunk, 2 * cols), BF16),
             pltpu.SemaphoreType.DMA((2, pos_v, 2)),
             pltpu.SemaphoreType.DMA((2, pos_v, 2)),
         ],

time: 107 us -> 96.5 us (0.902); the launches traced: 107 us -> 95.2 us
  Pallas kernels: 101 us -> 89.4 us
    pallas_call x1, Pallas kernels: 35.3 us -> 26.5 us  [on_device(): pl.pallas_call(functools.partial(line_kernel, pos_v), out_shape=jax.Shape...]
    pallas_call x1, Pallas kernels: 23.3 us -> 21.7 us  [on_device(): pl.pallas_call(functools.partial(gather_kernel, facets), out_shape=jax.Sh...]
    pallas_call x1, Pallas kernels: 6.04 us -> 4.73 us  [on_device(): pl.pallas_call(vis_kernel, out_shape=(jax.ShapeDtypeStruct((1, 2, slots),...]
where the time goes in v3:
time: 96.5 us; the launch traced here: 95.2 us
  Pallas kernels  89.4 us (93%)
  local copies, waits for them, and re-layouts  4.52 us (5%)
  between operations  1.31 us (1%)
    pallas_call x1, Pallas kernels, on_device(): pl.pallas_call(functools.partial(line_kernel, pos_v), out_shape=jax.Shape...  26.5 us
    pallas_call x1, Pallas kernels, on_device(): pl.pallas_call(functools.partial(gather_kernel, facets), out_shape=jax.Sh...  21.7 us
    pallas_call x1, Pallas kernels, on_device(): pl.pallas_call(functools.partial(halve_kernel, facets), out_shape=jax.Sha...  16.6 us
    pallas_call x1, Pallas kernels, on_device(): pl.pallas_call(functools.partial(transform_kernel, facets, pos_v), out_sh...  11.7 us
    pallas_call x1, Pallas kernels, on_device(): pl.pallas_call(functools.partial(adjoint_kernel, facets), out_shape=jax.S...  8.26 us
    pallas_call x1, Pallas kernels, on_device(): pl.pallas_call(vis_kernel, out_shape=(jax.ShapeDtypeStruct((1, 2, slots),...  4.73 us
    unnamed x2, local copies, waits for them, and re-layouts  4.52 us

profile of v3, /device:TPU:8, one launch (start us, length us, event | category | flops | bytes accessed | tf_op | source)
XLA Modules:
  0.0 95.2 jit_solution(10900867199242116797)
XLA Ops:
  0.6 2.5 %copy.10.spec = bf16[1,2,704,448]{3,2,1,0:T(8,128)(2,1)} copy(bf16[1,2,704,448]{2,3,1,0:T(8,128)(2,1)} %param.8) | data formatting | bytes 2523136 | tf_op args[0]
  3.1 11.7 %transform.1 = (bf16[8,2,256,256]{3,2,1,0:T(8,128)(2,1)}, bf16[512,512]{1,0:T(8,128)(2,1)}, bf16[640,512]{1,0:T(8,128)(2,1)}, bf16[640,512]{1,0:T(8,128)(2,1)}, s32[2,8]{1,0:T(2,128)}) custom-call(f32[2,256,256]{2,1,0:T(8,128)} %constant.4.clone.base, f32[8,2,256]{2,1,0:T(2,128)} %constant.11.turns, s32[32]{0:T(128)} %worker.1, ...), custom_call_target="tpu_custom_call" | custom-call | tf_op jit(solution)/shard_map/transform/pallas_call | solution.py:363
  14.8 16.6 %sum_grids.1.grid = bf16[2,256,256]{2,1,0:T(8,128)(2,1)} custom-call(bf16[8,2,256,256]{3,2,1,0:T(8,128)(2,1)} %get-tuple-element.9.slabs), custom_call_target="tpu_custom_call" | custom-call | tf_op jit(solution)/shard_map/sum_grids/pallas_call | solution.py:382
  32.1 4.7 %visibilities.1 = (f32[1,2,8192]{2,1,0:T(2,128)}, bf16[2,256,256]{2,1,0:T(8,128)(2,1)}) custom-call(s32[1]{0:T(128)S(6)} %copy.12.count, bf16[2,256,256]{2,1,0:T(8,128)(2,1)} %sum_grids.1.grid, s32[1,2,8192]{2,1,0:T(2,128)} %offsets.1, f32[1,2,8192]{2,1,0:T(2,128)} %fractions.1, f32[1,2,8192]{2,1,0:T(2,128)} %observed.1), custom_call_target="tpu_custom_call" | custom-call | tf_op jit(solution)/shard_map/visibilities/pallas_call | solution.py:399
  36.8 21.7 %gather_grids.1.everyone = bf16[8,2,256,256]{3,2,1,0:T(8,128)(2,1)} custom-call(bf16[2,256,256]{2,1,0:T(8,128)(2,1)} %get-tuple-element.12.own), custom_call_target="tpu_custom_call" | custom-call | tf_op jit(solution)/shard_map/gather_grids/pallas_call | solution.py:415
  58.5 8.3 %adjoint.1.pieces = bf16[4,176,896]{2,1,0:T(8,128)(2,1)} custom-call(s32[2,8]{1,0:T(2,128)} %get-tuple-element.11.corners, bf16[8,2,256,256]{3,2,1,0:T(8,128)(2,1)} %gather_grids.1.everyone, bf16[512,512]{1,0:T(8,128)(2,1)} %get-tuple-element.13.left_table, bf16[640,512]{1,0:T(8,128)(2,1)} %get-tuple-element.14.right_table, ...), custom_call_target="tpu_custom_call" | custom-call | tf_op jit(solution)/shard_map/adjoint/pallas_call | solution.py:431
  66.7 26.5 %sum_pieces.1 = f32[1,2,176,448]{3,2,1,0:T(8,128)} custom-call(bf16[4,176,896]{2,1,0:T(8,128)(2,1)} %adjoint.1.pieces), custom_call_target="tpu_custom_call" | custom-call | tf_op jit(solution)/shard_map/sum_pieces/pallas_call | solution.py:441
  93.2 2.0 %copy.13 = f32[1,2,176,448]{3,2,1,0:T(8,128)} copy(f32[1,2,176,448]{3,2,1,0:T(8,128)} %sum_pieces.1) | data formatting | bytes 1261568
